TPU v7x, 512 devices: a whole 4x8x8 slice. The times are simulated.
512 devices in a mesh: orb: 32 (over z, y_lo, core), dom: 16 (over x, y_hi).
Axes of the slice: x: 4, y: 8 (y_hi: 4, y_lo: 2; y = y_hi * 2 + y_lo), z: 8, core: 2. Of those that a mesh axis runs over, the one named last changes fastest.
Arguments:
- orbitals: bfloat16 [32, 16, 192, 128], P('orb', None, 'dom'), may hold values from -6 to 6
- potential: float32 [16, 192, 128], P(None, 'dom'), may hold values from 0 to 2
- degree: int32 [32], P('orb'), may hold values from 1 to 8, as said below
- owners: int32 [4], replicated, may hold values from 0 to 31
- rotation: bfloat16 [4, 1, 32], P(None, None, 'orb'), may hold values from -3 to 3
Outputs:
- filtered: float32 [32, 16, 192, 128], P('orb', None, 'dom')
- rotated: float32 [32, 16, 192, 128], P('orb', None, 'dom')
Inputs may be any that keep to these rules, and one draw needn't show every extreme that they name: Every draw has an orbital of degree 8 and one of degree 1. `owners`: panel numbers; panel q holds orbital q alone.
All inputs are finite; a program needn't handle non-finite values.
Results may differ from a plain program's by a relative error of at most 0.0003.
Values sent between devices are 32-bit elements; how exact they have to be, the bound alone decides.
A program may use at most 64 MiB of HBM per device.

v0:
```python
import jax
import jax.numpy as jnp
from jax import lax
from jax.sharding import PartitionSpec as P

RADIUS = 6
MAXDEG = 8
STEPS = 4
STENCIL = (
    -5369.0 / 1800.0,
    12.0 / 7.0,
    -15.0 / 56.0,
    10.0 / 189.0,
    -1.0 / 112.0,
    2.0 / 1925.0,
    -1.0 / 16632.0,
)
FILTER_CENTER = 7.75
FILTER_HALF = 6.25


def padded_2(block, sides, width):
    for axis, dim in sides:
        count = lax.axis_size(axis)
        forward = [(i, i + 1) for i in range(count - 1)]
        backward = [(target, source) for source, target in forward]
        low = lax.ppermute(
            lax.slice_in_dim(block, block.shape[dim] - width, None, axis=dim), axis, forward
        )
        high = lax.ppermute(lax.slice_in_dim(block, 0, width, axis=dim), axis, backward)
        block = jnp.concatenate([low, block, high], axis=dim)
    return block


def from_root(shard, axis, root):
    mine = lax.axis_index(axis) == root
    return lax.psum(jnp.where(mine, shard, jnp.zeros_like(shard)), axis)


def apply_hamiltonian(padded, potential):
    width = padded.shape[2] - 2 * RADIUS
    center = padded[:, :, RADIUS : RADIUS + width]
    laplace = 3.0 * STENCIL[0] * center
    for offset in range(1, RADIUS + 1):
        beside = (
            padded[:, :, RADIUS + offset : RADIUS + offset + width]
            + padded[:, :, RADIUS - offset : RADIUS - offset + width]
        )
        beside = beside + jnp.roll(center, offset, 3) + jnp.roll(center, -offset, 3)
        beside = beside + jnp.roll(center, offset, 1) + jnp.roll(center, -offset, 1)
        laplace = laplace + STENCIL[offset] * beside
    return -0.5 * laplace + potential * center


def chebyshev_next(applied, current, previous, first):
    shifted = applied - FILTER_CENTER * current
    if first:
        return shifted / FILTER_HALF
    return 2.0 / FILTER_HALF * shifted - previous


def keep_degree(selected, advanced, degree, level):
    return jnp.where((degree == level)[:, None, None, None], advanced, selected)


def per_device(orbitals, potential, degree, owners, rotation):
    block_rows = orbitals.shape[0]
    current = orbitals.astype(jnp.float32)
    previous = current
    selected = jnp.zeros_like(current)
    for section in range(MAXDEG):
        padded = padded_2(current, (("dom", 2),), RADIUS)
        applied = apply_hamiltonian(padded, potential)
        advanced = chebyshev_next(applied, current, previous, section == 0)
        selected = keep_degree(selected, advanced, degree, section + 1)
        previous, current = (current, advanced)
    flattened = selected.reshape(block_rows, -1)
    rotated = jnp.zeros(flattened.shape, jnp.float32)
    for section in range(STEPS):
        panel_block = from_root(flattened, "orb", owners[section])
        coefficients = rotation[section].astype(jnp.float32)
        rotated = rotated + lax.dot_general(
            coefficients,
            panel_block,
            (((0,), (0,)), ((), ())),
            precision=lax.Precision.HIGHEST,
            preferred_element_type=jnp.float32,
        )
    rotated = rotated.reshape(selected.shape)
    return (selected, rotated)


def solution(mesh):
    placed = (
        P("orb", None, "dom", None),
        P(None, "dom", None),
        P("orb"),
        P(),
        P(None, None, "orb"),
    )
    return jax.shard_map(
        per_device,
        mesh=mesh,
        in_specs=placed,
        out_specs=(P("orb", None, "dom", None), P("orb", None, "dom", None)),
        check_vma=False,
    )
```

profile of v0, /device:TPU:1, one launch (start us, length us, event | category | flops | bytes accessed | tf_op | source)
XLA Modules:
  0.0 363.2 jit_solution(5902551951845159628)
XLA Ops:
  7.2 1.4 fusion.652
  8.7 1.3 collective-permute-start
  10.0 6.3 %collective-permute-start.1 = (f32[1,16,6,128]{3,1,2,0:T(8,128)}, f32[1,16,6,128]{3,1,2,0:T(8,128)}, u32[]{:S(2)}, u32[]{:S(2)}) collective-permute-start(f32[1,16,6,128]{3,1,2,0:T(8,128)} %get-tuple-element.406), channel_id=1, source_target_pairs={{0,1},{1,2},{2,3},{3,4},{4,5},{5,6},{6,7},{7,8},{8,9},{9,10},{10,1... | collective-permute-start | bytes 147464 | tf_op jit(solution)/shard_map/ppermute | solution.py:27
  27.2 1.8 broadcast_multiply_fusion
  30.4 1.3 collective-permute-start.2
  31.7 5.5 %collective-permute-start.3 = (f32[1,16,6,128]{3,1,2,0:T(8,128)S(1)}, f32[1,16,6,128]{3,1,2,0:T(8,128)S(1)}, u32[]{:S(2)}, u32[]{:S(2)}) collective-permute-start(f32[1,16,6,128]{3,1,2,0:T(8,128)S(1)} %get-tuple-element.364), channel_id=1, source_target_pairs={{0,1},{1,2},{2,3},{3,4},{4,5},{5,6},{6,7},{7,8},{8,9},{9,10},{10,1... | collective-permute-start | bytes 147464 | tf_op jit(solution)/shard_map/ppermute | solution.py:27
  37.2 1.1 collective-permute-done.3
  40.4 1.3 collective-permute-start.4
  41.7 6.1 %collective-permute-start.5 = (f32[1,16,6,128]{3,1,2,0:T(8,128)S(1)}, f32[1,16,6,128]{3,1,2,0:T(8,128)S(1)}, u32[]{:S(2)}, u32[]{:S(2)}) collective-permute-start(f32[1,16,6,128]{3,1,2,0:T(8,128)S(1)} %get-tuple-element.314), channel_id=1, source_target_pairs={{0,1},{1,2},{2,3},{3,4},{4,5},{5,6},{6,7},{7,8},{8,9},{9,10},{10,1... | collective-permute-start | bytes 147464 | tf_op jit(solution)/shard_map/ppermute | solution.py:27
  47.8 1.1 collective-permute-done.5
  51.0 1.3 collective-permute-start.6
  52.3 6.9 %collective-permute-start.7 = (f32[1,16,6,128]{3,1,2,0:T(8,128)S(1)}, f32[1,16,6,128]{3,1,2,0:T(8,128)S(1)}, u32[]{:S(2)}, u32[]{:S(2)}) collective-permute-start(f32[1,16,6,128]{3,1,2,0:T(8,128)S(1)} %get-tuple-element.264), channel_id=1, source_target_pairs={{0,1},{1,2},{2,3},{3,4},{4,5},{5,6},{6,7},{7,8},{8,9},{9,10},{10,1... | collective-permute-start | bytes 147464 | tf_op jit(solution)/shard_map/ppermute | solution.py:27
  59.2 1.1 collective-permute-done.7
  62.4 1.3 collective-permute-start.8
  63.7 6.5 %collective-permute-start.9 = (f32[1,16,6,128]{3,1,2,0:T(8,128)S(1)}, f32[1,16,6,128]{3,1,2,0:T(8,128)S(1)}, u32[]{:S(2)}, u32[]{:S(2)}) collective-permute-start(f32[1,16,6,128]{3,1,2,0:T(8,128)S(1)} %get-tuple-element.214), channel_id=1, source_target_pairs={{0,1},{1,2},{2,3},{3,4},{4,5},{5,6},{6,7},{7,8},{8,9},{9,10},{10,1... | collective-permute-start | bytes 147464 | tf_op jit(solution)/shard_map/ppermute | solution.py:27
  70.2 1.1 collective-permute-done.9
  73.4 1.3 collective-permute-start.10
  74.7 6.4 %collective-permute-start.11 = (f32[1,16,6,128]{3,1,2,0:T(8,128)S(1)}, f32[1,16,6,128]{3,1,2,0:T(8,128)S(1)}, u32[]{:S(2)}, u32[]{:S(2)}) collective-permute-start(f32[1,16,6,128]{3,1,2,0:T(8,128)S(1)} %get-tuple-element.164), channel_id=1, source_target_pairs={{0,1},{1,2},{2,3},{3,4},{4,5},{5,6},{6,7},{7,8},{8,9},{9,10},{10,1... | collective-permute-start | bytes 147464 | tf_op jit(solution)/shard_map/ppermute | solution.py:27
  81.1 1.1 collective-permute-done.11
  84.3 1.3 collective-permute-start.12
  85.6 6.4 %collective-permute-start.13 = (f32[1,16,6,128]{3,1,2,0:T(8,128)S(1)}, f32[1,16,6,128]{3,1,2,0:T(8,128)S(1)}, u32[]{:S(2)}, u32[]{:S(2)}) collective-permute-start(f32[1,16,6,128]{3,1,2,0:T(8,128)S(1)} %get-tuple-element.114), channel_id=1, source_target_pairs={{0,1},{1,2},{2,3},{3,4},{4,5},{5,6},{6,7},{7,8},{8,9},{9,10},{10,1... | collective-permute-start | bytes 147464 | tf_op jit(solution)/shard_map/ppermute | solution.py:27
  92.0 1.1 collective-permute-done.13
  95.2 1.3 collective-permute-start.14
  96.5 6.7 %collective-permute-start.15 = (f32[1,16,6,128]{3,1,2,0:T(8,128)S(1)}, f32[1,16,6,128]{3,1,2,0:T(8,128)S(1)}, u32[]{:S(2)}, u32[]{:S(2)}) collective-permute-start(f32[1,16,6,128]{3,1,2,0:T(8,128)S(1)} %get-tuple-element.56), channel_id=1, source_target_pairs={{0,1},{1,2},{2,3},{3,4},{4,5},{5,6},{6,7},{7,8},{8,9},{9,10},{10,1... | collective-permute-start | bytes 147464 | tf_op jit(solution)/shard_map/ppermute | solution.py:27
  103.3 1.5 collective-permute-done.15
  104.8 0.7 broadcast_select_fusion.3
  106.2 0.7 select_n.108
  106.9 0.7 select_n.111
  107.7 0.7 select_n.114
  108.5 0.7 select_n.105
  112.4 241.8 %all-reduce.3.cloned.1.call-done = (f32[1,24576]{1,0:T(1,128)}, f32[1,24576]{1,0:T(1,128)}, f32[1,24576]{1,0:T(1,128)}, f32[1,24576]{1,0:T(1,128)}) async-done(((f32[1,24576]{1,0:T(1,128)}, f32[1,24576]{1,0:T(1,128)}, f32[1,24576]{1,0:T(1,128)}, f32[1,24576]{1,0:T(1,128)}), (f32[1,24576]{1,0:T(1,128)}, f32[1,24576]{1,0:T(1,128)}, f32[1,24576]{1,0:T(1,128)}, ...) | async-done | bytes 393232 | tf_op jit(solution)/shard_map/psum | solution.py:37
  354.2 1.4 add_reduce_fusion
  (242 shorter events, 22.2 us)
Async XLA Ops:
  7.2 347.0 %all-reduce.3.cloned.1.call-start = ((), (), s32[]{:S(2)}) async-start(), calls=%async_computation | async-start | bytes 786432 | tf_op jit(solution)/shard_map/psum | solution.py:37
  7.2 9.0 %copy-start = (bf16[1,16,12,128]{3,1,2,0:T(8,128)(2,1)S(1)}, bf16[1,16,12,128]{3,1,2,0:T(8,128)(2,1)}, u32[]{:S(2)}) copy-start(bf16[1,16,12,128]{3,1,2,0:T(8,128)(2,1)} %param.5) | copy-start | bytes 147460
  8.7 17.8 %collective-permute-start = (f32[1,16,6,128]{3,1,2,0:T(8,128)}, f32[1,16,6,128]{3,1,2,0:T(8,128)}, u32[]{:S(2)}, u32[]{:S(2)}) collective-permute-start(f32[1,16,6,128]{3,1,2,0:T(8,128)} %get-tuple-element.405), channel_id=1, source_target_pairs={{1,0},{2,1},{3,2},{4,3},{5,4},{6,5},{7,6},{8,7},{9,8},{10,9},{11,1... | collective-permute-start | bytes 147464 | tf_op jit(solution)/shard_map/ppermute | solution.py:30
  10.0 16.5 %collective-permute-start.1 = (f32[1,16,6,128]{3,1,2,0:T(8,128)}, f32[1,16,6,128]{3,1,2,0:T(8,128)}, u32[]{:S(2)}, u32[]{:S(2)}) collective-permute-start(f32[1,16,6,128]{3,1,2,0:T(8,128)} %get-tuple-element.406), channel_id=1, source_target_pairs={{0,1},{1,2},{2,3},{3,4},{4,5},{5,6},{6,7},{7,8},{8,9},{9,10},{10,1... | collective-permute-start | bytes 147464 | tf_op jit(solution)/shard_map/ppermute | solution.py:27
  20.6 1.8 copy-start.6
  23.2 3.3 copy-start.1
  26.5 0.7 copy-start.3
  26.5 0.7 copy-start.4
  26.5 0.7 copy-start.5
  30.4 6.8 %collective-permute-start.2 = (f32[1,16,6,128]{3,1,2,0:T(8,128)S(1)}, f32[1,16,6,128]{3,1,2,0:T(8,128)S(1)}, u32[]{:S(2)}, u32[]{:S(2)}) collective-permute-start(f32[1,16,6,128]{3,1,2,0:T(8,128)S(1)} %get-tuple-element.363), channel_id=1, source_target_pairs={{1,0},{2,1},{3,2},{4,3},{5,4},{6,5},{7,6},{8,7},{9,8},{10,9},{11,1... | collective-permute-start | bytes 147464 | tf_op jit(solution)/shard_map/ppermute | solution.py:30
  31.7 6.7 %collective-permute-start.3 = (f32[1,16,6,128]{3,1,2,0:T(8,128)S(1)}, f32[1,16,6,128]{3,1,2,0:T(8,128)S(1)}, u32[]{:S(2)}, u32[]{:S(2)}) collective-permute-start(f32[1,16,6,128]{3,1,2,0:T(8,128)S(1)} %get-tuple-element.364), channel_id=1, source_target_pairs={{0,1},{1,2},{2,3},{3,4},{4,5},{5,6},{6,7},{7,8},{8,9},{9,10},{10,1... | collective-permute-start | bytes 147464 | tf_op jit(solution)/shard_map/ppermute | solution.py:27
  40.4 7.4 %collective-permute-start.4 = (f32[1,16,6,128]{3,1,2,0:T(8,128)S(1)}, f32[1,16,6,128]{3,1,2,0:T(8,128)S(1)}, u32[]{:S(2)}, u32[]{:S(2)}) collective-permute-start(f32[1,16,6,128]{3,1,2,0:T(8,128)S(1)} %get-tuple-element.313), channel_id=1, source_target_pairs={{1,0},{2,1},{3,2},{4,3},{5,4},{6,5},{7,6},{8,7},{9,8},{10,9},{11,1... | collective-permute-start | bytes 147464 | tf_op jit(solution)/shard_map/ppermute | solution.py:30
  41.7 7.3 %collective-permute-start.5 = (f32[1,16,6,128]{3,1,2,0:T(8,128)S(1)}, f32[1,16,6,128]{3,1,2,0:T(8,128)S(1)}, u32[]{:S(2)}, u32[]{:S(2)}) collective-permute-start(f32[1,16,6,128]{3,1,2,0:T(8,128)S(1)} %get-tuple-element.314), channel_id=1, source_target_pairs={{0,1},{1,2},{2,3},{3,4},{4,5},{5,6},{6,7},{7,8},{8,9},{9,10},{10,1... | collective-permute-start | bytes 147464 | tf_op jit(solution)/shard_map/ppermute | solution.py:27
  51.0 8.3 %collective-permute-start.6 = (f32[1,16,6,128]{3,1,2,0:T(8,128)S(1)}, f32[1,16,6,128]{3,1,2,0:T(8,128)S(1)}, u32[]{:S(2)}, u32[]{:S(2)}) collective-permute-start(f32[1,16,6,128]{3,1,2,0:T(8,128)S(1)} %get-tuple-element.263), channel_id=1, source_target_pairs={{1,0},{2,1},{3,2},{4,3},{5,4},{6,5},{7,6},{8,7},{9,8},{10,9},{11,1... | collective-permute-start | bytes 147464 | tf_op jit(solution)/shard_map/ppermute | solution.py:30
  52.3 8.1 %collective-permute-start.7 = (f32[1,16,6,128]{3,1,2,0:T(8,128)S(1)}, f32[1,16,6,128]{3,1,2,0:T(8,128)S(1)}, u32[]{:S(2)}, u32[]{:S(2)}) collective-permute-start(f32[1,16,6,128]{3,1,2,0:T(8,128)S(1)} %get-tuple-element.264), channel_id=1, source_target_pairs={{0,1},{1,2},{2,3},{3,4},{4,5},{5,6},{6,7},{7,8},{8,9},{9,10},{10,1... | collective-permute-start | bytes 147464 | tf_op jit(solution)/shard_map/ppermute | solution.py:27
  62.4 7.8 %collective-permute-start.8 = (f32[1,16,6,128]{3,1,2,0:T(8,128)S(1)}, f32[1,16,6,128]{3,1,2,0:T(8,128)S(1)}, u32[]{:S(2)}, u32[]{:S(2)}) collective-permute-start(f32[1,16,6,128]{3,1,2,0:T(8,128)S(1)} %get-tuple-element.213), channel_id=1, source_target_pairs={{1,0},{2,1},{3,2},{4,3},{5,4},{6,5},{7,6},{8,7},{9,8},{10,9},{11,1... | collective-permute-start | bytes 147464 | tf_op jit(solution)/shard_map/ppermute | solution.py:30
  63.7 7.6 %collective-permute-start.9 = (f32[1,16,6,128]{3,1,2,0:T(8,128)S(1)}, f32[1,16,6,128]{3,1,2,0:T(8,128)S(1)}, u32[]{:S(2)}, u32[]{:S(2)}) collective-permute-start(f32[1,16,6,128]{3,1,2,0:T(8,128)S(1)} %get-tuple-element.214), channel_id=1, source_target_pairs={{0,1},{1,2},{2,3},{3,4},{4,5},{5,6},{6,7},{7,8},{8,9},{9,10},{10,1... | collective-permute-start | bytes 147464 | tf_op jit(solution)/shard_map/ppermute | solution.py:27
  73.4 7.7 %collective-permute-start.10 = (f32[1,16,6,128]{3,1,2,0:T(8,128)S(1)}, f32[1,16,6,128]{3,1,2,0:T(8,128)S(1)}, u32[]{:S(2)}, u32[]{:S(2)}) collective-permute-start(f32[1,16,6,128]{3,1,2,0:T(8,128)S(1)} %get-tuple-element.163), channel_id=1, source_target_pairs={{1,0},{2,1},{3,2},{4,3},{5,4},{6,5},{7,6},{8,7},{9,8},{10,9},{11,1... | collective-permute-start | bytes 147464 | tf_op jit(solution)/shard_map/ppermute | solution.py:30
  74.7 7.6 %collective-permute-start.11 = (f32[1,16,6,128]{3,1,2,0:T(8,128)S(1)}, f32[1,16,6,128]{3,1,2,0:T(8,128)S(1)}, u32[]{:S(2)}, u32[]{:S(2)}) collective-permute-start(f32[1,16,6,128]{3,1,2,0:T(8,128)S(1)} %get-tuple-element.164), channel_id=1, source_target_pairs={{0,1},{1,2},{2,3},{3,4},{4,5},{5,6},{6,7},{7,8},{8,9},{9,10},{10,1... | collective-permute-start | bytes 147464 | tf_op jit(solution)/shard_map/ppermute | solution.py:27
  84.3 7.7 %collective-permute-start.12 = (f32[1,16,6,128]{3,1,2,0:T(8,128)S(1)}, f32[1,16,6,128]{3,1,2,0:T(8,128)S(1)}, u32[]{:S(2)}, u32[]{:S(2)}) collective-permute-start(f32[1,16,6,128]{3,1,2,0:T(8,128)S(1)} %get-tuple-element.113), channel_id=1, source_target_pairs={{1,0},{2,1},{3,2},{4,3},{5,4},{6,5},{7,6},{8,7},{9,8},{10,9},{11,1... | collective-permute-start | bytes 147464 | tf_op jit(solution)/shard_map/ppermute | solution.py:30
  85.6 7.6 %collective-permute-start.13 = (f32[1,16,6,128]{3,1,2,0:T(8,128)S(1)}, f32[1,16,6,128]{3,1,2,0:T(8,128)S(1)}, u32[]{:S(2)}, u32[]{:S(2)}) collective-permute-start(f32[1,16,6,128]{3,1,2,0:T(8,128)S(1)} %get-tuple-element.114), channel_id=1, source_target_pairs={{0,1},{1,2},{2,3},{3,4},{4,5},{5,6},{6,7},{7,8},{8,9},{9,10},{10,1... | collective-permute-start | bytes 147464 | tf_op jit(solution)/shard_map/ppermute | solution.py:27
  95.2 8.1 %collective-permute-start.14 = (f32[1,16,6,128]{3,1,2,0:T(8,128)S(1)}, f32[1,16,6,128]{3,1,2,0:T(8,128)S(1)}, u32[]{:S(2)}, u32[]{:S(2)}) collective-permute-start(f32[1,16,6,128]{3,1,2,0:T(8,128)S(1)} %get-tuple-element.55), channel_id=1, source_target_pairs={{1,0},{2,1},{3,2},{4,3},{5,4},{6,5},{7,6},{8,7},{9,8},{10,9},{11,1... | collective-permute-start | bytes 147464 | tf_op jit(solution)/shard_map/ppermute | solution.py:30
  96.5 8.2 %collective-permute-start.15 = (f32[1,16,6,128]{3,1,2,0:T(8,128)S(1)}, f32[1,16,6,128]{3,1,2,0:T(8,128)S(1)}, u32[]{:S(2)}, u32[]{:S(2)}) collective-permute-start(f32[1,16,6,128]{3,1,2,0:T(8,128)S(1)} %get-tuple-element.56), channel_id=1, source_target_pairs={{0,1},{1,2},{2,3},{3,4},{4,5},{5,6},{6,7},{7,8},{8,9},{9,10},{10,1... | collective-permute-start | bytes 147464 | tf_op jit(solution)/shard_map/ppermute | solution.py:27
  105.5 0.6 copy-start.2
  107.7 1.5 copy-start.7
Sparse Core Ops, SparseCore 0:
  109.4 244.7 all-reduce.2
where the time goes:
time: 364 us; the launch traced here: 363 us
  waiting for transfers between devices  250 us (69%)
  starting transfers between devices  61.2 us (17%)
  local copies, waits for them, and re-layouts  22.4 us (6%)
  between operations  21.5 us (6%)
  other arithmetic  8.01 us (2%)
    psum x1, waiting for transfers between devices, from_root(): return lax.psum(jnp.where(mine, shard, jnp.zeros_like(shard)), axis)  242 us
    ppermute x8, starting transfers between devices, padded_2(): lax.ppermute(lax.slice_in_dim(block, block.shape[dim] - width, None, axis...  50.8 us
    ppermute x8, starting transfers between devices, padded_2(): lax.ppermute(lax.slice_in_dim(block, 0, width, axis=dim), axis, backward)  10.3 us
    slice x96, local copies, waits for them, and re-layouts, apply_hamiltonian(): beside = beside + jnp.roll(center, offset, 3) + jnp.roll(center, -offset, 3)  8.87 us
    ppermute x8, waiting for transfers between devices, padded_2(): lax.ppermute(lax.slice_in_dim(block, block.shape[dim] - width, None, axis...  8.25 us
  transfers between devices with their start and end apart: 17, of which 8 were waited for; matrix products, arithmetic and copies ran while one was open for 2% of the time, Pallas kernels for 0%

commit v1 on v0

--- a/solution.py
+++ b/solution.py
@@ -34,7 +34,7 @@
 
 def from_root(shard, axis, root):
     mine = lax.axis_index(axis) == root
-    return lax.psum(jnp.where(mine, shard, jnp.zeros_like(shard)), axis)
+    return jnp.sum(lax.all_gather(jnp.where(mine, shard, jnp.zeros_like(shard)), axis), axis=0)
 
 
 def apply_hamiltonian(padded, potential):

time: 364 us -> 432 us (1.19)
  waiting for transfers between devices: 250 us -> 297 us
  other arithmetic: 8.01 us -> 22.5 us
  local copies, waits for them, and re-layouts: 22.4 us -> 28.1 us
    all_gather x0 -> x4, waiting for transfers between devices: none -> 289 us  [from_root(): lax.all_gather(jnp.where(mine, shard, jnp.zeros_like(shard)), axis)]
    psum x1 -> x0, waiting for transfers between devices: 242 us -> none  [from_root(): return lax.psum(jnp.where(mine, shard, jnp.zeros_like(shard)), axis)]
    reduce_sum x0 -> x4, other arithmetic: none -> 15.7 us  [from_root(): jnp.sum(lax.all_gather(jnp.where(mine, shard, jnp.zeros_like(shard)), axi...]
    slice x96, local copies, waits for them, and re-layouts: 8.87 us -> 14.1 us  [apply_hamiltonian(): beside = beside + jnp.roll(center, offset, 3) + jnp.roll(center, -offset, 3)]
  transfers between devices with their start and end apart: 17 -> 20, of which waited for: 8 -> 11; matrix products, arithmetic and copies ran while one was open for 2% -> 7% of each run, Pallas kernels for 0% -> 0%
where the time goes in v1:
time: 432 us; the launch traced here: 431 us
  waiting for transfers between devices  297 us (69%)
  starting transfers between devices  61.5 us (14%)
  local copies, waits for them, and re-layouts  28.1 us (7%)
  other arithmetic  22.5 us (5%)
  between operations  21.2 us (5%)
    all_gather x4, waiting for transfers between devices, from_root(): lax.all_gather(jnp.where(mine, shard, jnp.zeros_like(shard)), axis)  289 us
    ppermute x8, starting transfers between devices, padded_2(): lax.ppermute(lax.slice_in_dim(block, block.shape[dim] - width, None, axis...  51 us
    reduce_sum x4, other arithmetic, from_root(): jnp.sum(lax.all_gather(jnp.where(mine, shard, jnp.zeros_like(shard)), axi...  15.7 us
    slice x96, local copies, waits for them, and re-layouts, apply_hamiltonian(): beside = beside + jnp.roll(center, offset, 3) + jnp.roll(center, -offset, 3)  14.1 us
    ppermute x8, starting transfers between devices, padded_2(): lax.ppermute(lax.slice_in_dim(block, 0, width, axis=dim), axis, backward)  10.3 us
  transfers between devices with their start and end apart: 20, of which 11 were waited for; matrix products, arithmetic and copies ran while one was open for 7% of the time, Pallas kernels for 0%

profile of v1, /device:TPU:1, one launch (start us, length us, event | category | flops | bytes accessed | tf_op | source)
XLA Modules:
  0.0 430.8 jit_solution(2391849489792869376)
XLA Ops:
  7.2 1.4 fusion.652
  8.6 1.3 collective-permute-start
  9.9 6.3 %collective-permute-start.1 = (f32[1,16,6,128]{3,1,2,0:T(8,128)}, f32[1,16,6,128]{3,1,2,0:T(8,128)}, u32[]{:S(2)}, u32[]{:S(2)}) collective-permute-start(f32[1,16,6,128]{3,1,2,0:T(8,128)} %get-tuple-element.404), channel_id=1, source_target_pairs={{0,1},{1,2},{2,3},{3,4},{4,5},{5,6},{6,7},{7,8},{8,9},{9,10},{10,1... | collective-permute-start | bytes 147464 | tf_op jit(solution)/shard_map/ppermute | solution.py:27
  33.4 1.9 broadcast_multiply_fusion
  36.7 1.3 collective-permute-start.2
  38.0 5.5 %collective-permute-start.3 = (f32[1,16,6,128]{3,1,2,0:T(8,128)S(1)}, f32[1,16,6,128]{3,1,2,0:T(8,128)S(1)}, u32[]{:S(2)}, u32[]{:S(2)}) collective-permute-start(f32[1,16,6,128]{3,1,2,0:T(8,128)S(1)} %get-tuple-element.362), channel_id=1, source_target_pairs={{0,1},{1,2},{2,3},{3,4},{4,5},{5,6},{6,7},{7,8},{8,9},{9,10},{10,1... | collective-permute-start | bytes 147464 | tf_op jit(solution)/shard_map/ppermute | solution.py:27
  43.5 1.1 collective-permute-done.3
  46.7 1.3 collective-permute-start.4
  48.0 6.1 %collective-permute-start.5 = (f32[1,16,6,128]{3,1,2,0:T(8,128)S(1)}, f32[1,16,6,128]{3,1,2,0:T(8,128)S(1)}, u32[]{:S(2)}, u32[]{:S(2)}) collective-permute-start(f32[1,16,6,128]{3,1,2,0:T(8,128)S(1)} %get-tuple-element.312), channel_id=1, source_target_pairs={{0,1},{1,2},{2,3},{3,4},{4,5},{5,6},{6,7},{7,8},{8,9},{9,10},{10,1... | collective-permute-start | bytes 147464 | tf_op jit(solution)/shard_map/ppermute | solution.py:27
  54.1 1.1 collective-permute-done.5
  57.3 1.3 collective-permute-start.6
  58.6 6.9 %collective-permute-start.7 = (f32[1,16,6,128]{3,1,2,0:T(8,128)S(1)}, f32[1,16,6,128]{3,1,2,0:T(8,128)S(1)}, u32[]{:S(2)}, u32[]{:S(2)}) collective-permute-start(f32[1,16,6,128]{3,1,2,0:T(8,128)S(1)} %get-tuple-element.262), channel_id=1, source_target_pairs={{0,1},{1,2},{2,3},{3,4},{4,5},{5,6},{6,7},{7,8},{8,9},{9,10},{10,1... | collective-permute-start | bytes 147464 | tf_op jit(solution)/shard_map/ppermute | solution.py:27
  65.6 1.1 collective-permute-done.7
  68.8 1.3 collective-permute-start.8
  70.1 6.5 %collective-permute-start.9 = (f32[1,16,6,128]{3,1,2,0:T(8,128)S(1)}, f32[1,16,6,128]{3,1,2,0:T(8,128)S(1)}, u32[]{:S(2)}, u32[]{:S(2)}) collective-permute-start(f32[1,16,6,128]{3,1,2,0:T(8,128)S(1)} %get-tuple-element.212), channel_id=1, source_target_pairs={{0,1},{1,2},{2,3},{3,4},{4,5},{5,6},{6,7},{7,8},{8,9},{9,10},{10,1... | collective-permute-start | bytes 147464 | tf_op jit(solution)/shard_map/ppermute | solution.py:27
  76.6 1.1 collective-permute-done.9
  79.7 1.3 collective-permute-start.10
  81.0 6.4 %collective-permute-start.11 = (f32[1,16,6,128]{3,1,2,0:T(8,128)S(1)}, f32[1,16,6,128]{3,1,2,0:T(8,128)S(1)}, u32[]{:S(2)}, u32[]{:S(2)}) collective-permute-start(f32[1,16,6,128]{3,1,2,0:T(8,128)S(1)} %get-tuple-element.162), channel_id=1, source_target_pairs={{0,1},{1,2},{2,3},{3,4},{4,5},{5,6},{6,7},{7,8},{8,9},{9,10},{10,1... | collective-permute-start | bytes 147464 | tf_op jit(solution)/shard_map/ppermute | solution.py:27
  87.5 1.1 collective-permute-done.11
  90.7 1.3 collective-permute-start.12
  92.0 6.4 %collective-permute-start.13 = (f32[1,16,6,128]{3,1,2,0:T(8,128)S(1)}, f32[1,16,6,128]{3,1,2,0:T(8,128)S(1)}, u32[]{:S(2)}, u32[]{:S(2)}) collective-permute-start(f32[1,16,6,128]{3,1,2,0:T(8,128)S(1)} %get-tuple-element.112), channel_id=1, source_target_pairs={{0,1},{1,2},{2,3},{3,4},{4,5},{5,6},{6,7},{7,8},{8,9},{9,10},{10,1... | collective-permute-start | bytes 147464 | tf_op jit(solution)/shard_map/ppermute | solution.py:27
  101.6 1.3 collective-permute-start.14
  102.9 6.9 %collective-permute-start.15 = (f32[1,16,6,128]{3,1,2,0:T(8,128)S(1)}, f32[1,16,6,128]{3,1,2,0:T(8,128)S(1)}, u32[]{:S(2)}, u32[]{:S(2)}) collective-permute-start(f32[1,16,6,128]{3,1,2,0:T(8,128)S(1)} %get-tuple-element.54), channel_id=1, source_target_pairs={{0,1},{1,2},{2,3},{3,4},{4,5},{5,6},{6,7},{7,8},{8,9},{9,10},{10,1... | collective-permute-start | bytes 147464 | tf_op jit(solution)/shard_map/ppermute | solution.py:27
  109.8 1.3 collective-permute-done.15
  118.4 89.0 %all-gather.7.cloned.1.call-done = f32[32,1,24576]{2,1,0:T(1,128)} async-done(((f32[1,1,24576]{2,1,0:T(1,128)}), f32[32,1,24576]{2,1,0:T(1,128)}) %all-gather.7.cloned.1.call-update) | async-done | bytes 3145744 | tf_op jit(solution)/shard_map/all_gather | solution.py:37
  207.5 3.9 reduce_sum.37
  211.4 66.6 %all-gather.9.cloned.1.call-done = f32[32,1,24576]{2,1,0:T(1,128)} async-done(((f32[1,1,24576]{2,1,0:T(1,128)}), f32[32,1,24576]{2,1,0:T(1,128)}) %all-gather.9.cloned.1.call-update) | async-done | bytes 3145744 | tf_op jit(solution)/shard_map/all_gather | solution.py:37
  278.0 3.9 reduce_sum.38
  282.0 67.2 %all-gather.11.cloned.1.call-done = f32[32,1,24576]{2,1,0:T(1,128)} async-done(((f32[1,1,24576]{2,1,0:T(1,128)}), f32[32,1,24576]{2,1,0:T(1,128)}) %all-gather.11.cloned.1.call-update) | async-done | bytes 3145744 | tf_op jit(solution)/shard_map/all_gather | solution.py:37
  349.2 3.9 reduce_sum.39
  353.1 66.5 %all-gather.5.cloned.1.call-done = f32[32,1,24576]{2,1,0:T(1,128)} async-done(((f32[1,1,24576]{2,1,0:T(1,128)}), f32[32,1,24576]{2,1,0:T(1,128)}) %all-gather.5.cloned.1.call-update) | async-done | bytes 3145744 | tf_op jit(solution)/shard_map/all_gather | solution.py:37
  419.6 3.9 reduce_sum.36
  (249 shorter events, 33.0 us)
Async XLA Ops:
  7.2 16.6 %copy-start = (bf16[1,16,12,128]{3,1,2,0:T(8,128)(2,1)S(1)}, bf16[1,16,12,128]{3,1,2,0:T(8,128)(2,1)}, u32[]{:S(2)}) copy-start(bf16[1,16,12,128]{3,1,2,0:T(8,128)(2,1)} %param.5) | copy-start | bytes 147460
  7.2 200.3 %all-gather.7.cloned.1.call-start = ((), (), s32[]{:S(2)}) async-start(), calls=%async_computation.1 | async-start | bytes 3244032 | tf_op jit(solution)/shard_map/all_gather | solution.py:37
  8.6 24.8 %collective-permute-start = (f32[1,16,6,128]{3,1,2,0:T(8,128)}, f32[1,16,6,128]{3,1,2,0:T(8,128)}, u32[]{:S(2)}, u32[]{:S(2)}) collective-permute-start(f32[1,16,6,128]{3,1,2,0:T(8,128)} %get-tuple-element.403), channel_id=1, source_target_pairs={{1,0},{2,1},{3,2},{4,3},{5,4},{6,5},{7,6},{8,7},{9,8},{10,9},{11,1... | collective-permute-start | bytes 147464 | tf_op jit(solution)/shard_map/ppermute | solution.py:30
  9.9 23.5 %collective-permute-start.1 = (f32[1,16,6,128]{3,1,2,0:T(8,128)}, f32[1,16,6,128]{3,1,2,0:T(8,128)}, u32[]{:S(2)}, u32[]{:S(2)}) collective-permute-start(f32[1,16,6,128]{3,1,2,0:T(8,128)} %get-tuple-element.404), channel_id=1, source_target_pairs={{0,1},{1,2},{2,3},{3,4},{4,5},{5,6},{6,7},{7,8},{8,9},{9,10},{10,1... | collective-permute-start | bytes 147464 | tf_op jit(solution)/shard_map/ppermute | solution.py:27
  20.0 9.5 %copy-start.3 = (s32[4]{0:T(128)S(1)}, s32[4]{0:T(128)}, u32[]{:S(2)}) copy-start(s32[4]{0:T(128)} %param.8) | copy-start | bytes 52
  20.0 13.4 %copy-start.1 = (f32[16,12,128]{2,0,1:T(8,128)S(1)}, f32[16,12,128]{2,0,1:T(8,128)}, u32[]{:S(2)}) copy-start(f32[16,12,128]{2,0,1:T(8,128)} %param.6) | copy-start | bytes 294916
  36.7 6.8 %collective-permute-start.2 = (f32[1,16,6,128]{3,1,2,0:T(8,128)S(1)}, f32[1,16,6,128]{3,1,2,0:T(8,128)S(1)}, u32[]{:S(2)}, u32[]{:S(2)}) collective-permute-start(f32[1,16,6,128]{3,1,2,0:T(8,128)S(1)} %get-tuple-element.361), channel_id=1, source_target_pairs={{1,0},{2,1},{3,2},{4,3},{5,4},{6,5},{7,6},{8,7},{9,8},{10,9},{11,1... | collective-permute-start | bytes 147464 | tf_op jit(solution)/shard_map/ppermute | solution.py:30
  38.0 6.7 %collective-permute-start.3 = (f32[1,16,6,128]{3,1,2,0:T(8,128)S(1)}, f32[1,16,6,128]{3,1,2,0:T(8,128)S(1)}, u32[]{:S(2)}, u32[]{:S(2)}) collective-permute-start(f32[1,16,6,128]{3,1,2,0:T(8,128)S(1)} %get-tuple-element.362), channel_id=1, source_target_pairs={{0,1},{1,2},{2,3},{3,4},{4,5},{5,6},{6,7},{7,8},{8,9},{9,10},{10,1... | collective-permute-start | bytes 147464 | tf_op jit(solution)/shard_map/ppermute | solution.py:27
  46.7 7.4 %collective-permute-start.4 = (f32[1,16,6,128]{3,1,2,0:T(8,128)S(1)}, f32[1,16,6,128]{3,1,2,0:T(8,128)S(1)}, u32[]{:S(2)}, u32[]{:S(2)}) collective-permute-start(f32[1,16,6,128]{3,1,2,0:T(8,128)S(1)} %get-tuple-element.311), channel_id=1, source_target_pairs={{1,0},{2,1},{3,2},{4,3},{5,4},{6,5},{7,6},{8,7},{9,8},{10,9},{11,1... | collective-permute-start | bytes 147464 | tf_op jit(solution)/shard_map/ppermute | solution.py:30
  48.0 7.3 %collective-permute-start.5 = (f32[1,16,6,128]{3,1,2,0:T(8,128)S(1)}, f32[1,16,6,128]{3,1,2,0:T(8,128)S(1)}, u32[]{:S(2)}, u32[]{:S(2)}) collective-permute-start(f32[1,16,6,128]{3,1,2,0:T(8,128)S(1)} %get-tuple-element.312), channel_id=1, source_target_pairs={{0,1},{1,2},{2,3},{3,4},{4,5},{5,6},{6,7},{7,8},{8,9},{9,10},{10,1... | collective-permute-start | bytes 147464 | tf_op jit(solution)/shard_map/ppermute | solution.py:27
  57.3 8.3 %collective-permute-start.6 = (f32[1,16,6,128]{3,1,2,0:T(8,128)S(1)}, f32[1,16,6,128]{3,1,2,0:T(8,128)S(1)}, u32[]{:S(2)}, u32[]{:S(2)}) collective-permute-start(f32[1,16,6,128]{3,1,2,0:T(8,128)S(1)} %get-tuple-element.261), channel_id=1, source_target_pairs={{1,0},{2,1},{3,2},{4,3},{5,4},{6,5},{7,6},{8,7},{9,8},{10,9},{11,1... | collective-permute-start | bytes 147464 | tf_op jit(solution)/shard_map/ppermute | solution.py:30
  58.6 8.1 %collective-permute-start.7 = (f32[1,16,6,128]{3,1,2,0:T(8,128)S(1)}, f32[1,16,6,128]{3,1,2,0:T(8,128)S(1)}, u32[]{:S(2)}, u32[]{:S(2)}) collective-permute-start(f32[1,16,6,128]{3,1,2,0:T(8,128)S(1)} %get-tuple-element.262), channel_id=1, source_target_pairs={{0,1},{1,2},{2,3},{3,4},{4,5},{5,6},{6,7},{7,8},{8,9},{9,10},{10,1... | collective-permute-start | bytes 147464 | tf_op jit(solution)/shard_map/ppermute | solution.py:27
  68.8 7.8 %collective-permute-start.8 = (f32[1,16,6,128]{3,1,2,0:T(8,128)S(1)}, f32[1,16,6,128]{3,1,2,0:T(8,128)S(1)}, u32[]{:S(2)}, u32[]{:S(2)}) collective-permute-start(f32[1,16,6,128]{3,1,2,0:T(8,128)S(1)} %get-tuple-element.211), channel_id=1, source_target_pairs={{1,0},{2,1},{3,2},{4,3},{5,4},{6,5},{7,6},{8,7},{9,8},{10,9},{11,1... | collective-permute-start | bytes 147464 | tf_op jit(solution)/shard_map/ppermute | solution.py:30
  70.1 7.6 %collective-permute-start.9 = (f32[1,16,6,128]{3,1,2,0:T(8,128)S(1)}, f32[1,16,6,128]{3,1,2,0:T(8,128)S(1)}, u32[]{:S(2)}, u32[]{:S(2)}) collective-permute-start(f32[1,16,6,128]{3,1,2,0:T(8,128)S(1)} %get-tuple-element.212), channel_id=1, source_target_pairs={{0,1},{1,2},{2,3},{3,4},{4,5},{5,6},{6,7},{7,8},{8,9},{9,10},{10,1... | collective-permute-start | bytes 147464 | tf_op jit(solution)/shard_map/ppermute | solution.py:27
  79.7 7.7 %collective-permute-start.10 = (f32[1,16,6,128]{3,1,2,0:T(8,128)S(1)}, f32[1,16,6,128]{3,1,2,0:T(8,128)S(1)}, u32[]{:S(2)}, u32[]{:S(2)}) collective-permute-start(f32[1,16,6,128]{3,1,2,0:T(8,128)S(1)} %get-tuple-element.161), channel_id=1, source_target_pairs={{1,0},{2,1},{3,2},{4,3},{5,4},{6,5},{7,6},{8,7},{9,8},{10,9},{11,1... | collective-permute-start | bytes 147464 | tf_op jit(solution)/shard_map/ppermute | solution.py:30
  81.0 7.6 %collective-permute-start.11 = (f32[1,16,6,128]{3,1,2,0:T(8,128)S(1)}, f32[1,16,6,128]{3,1,2,0:T(8,128)S(1)}, u32[]{:S(2)}, u32[]{:S(2)}) collective-permute-start(f32[1,16,6,128]{3,1,2,0:T(8,128)S(1)} %get-tuple-element.162), channel_id=1, source_target_pairs={{0,1},{1,2},{2,3},{3,4},{4,5},{5,6},{6,7},{7,8},{8,9},{9,10},{10,1... | collective-permute-start | bytes 147464 | tf_op jit(solution)/shard_map/ppermute | solution.py:27
  90.7 7.7 %collective-permute-start.12 = (f32[1,16,6,128]{3,1,2,0:T(8,128)S(1)}, f32[1,16,6,128]{3,1,2,0:T(8,128)S(1)}, u32[]{:S(2)}, u32[]{:S(2)}) collective-permute-start(f32[1,16,6,128]{3,1,2,0:T(8,128)S(1)} %get-tuple-element.111), channel_id=1, source_target_pairs={{1,0},{2,1},{3,2},{4,3},{5,4},{6,5},{7,6},{8,7},{9,8},{10,9},{11,1... | collective-permute-start | bytes 147464 | tf_op jit(solution)/shard_map/ppermute | solution.py:30
  92.0 7.6 %collective-permute-start.13 = (f32[1,16,6,128]{3,1,2,0:T(8,128)S(1)}, f32[1,16,6,128]{3,1,2,0:T(8,128)S(1)}, u32[]{:S(2)}, u32[]{:S(2)}) collective-permute-start(f32[1,16,6,128]{3,1,2,0:T(8,128)S(1)} %get-tuple-element.112), channel_id=1, source_target_pairs={{0,1},{1,2},{2,3},{3,4},{4,5},{5,6},{6,7},{7,8},{8,9},{9,10},{10,1... | collective-permute-start | bytes 147464 | tf_op jit(solution)/shard_map/ppermute | solution.py:27
  101.6 8.2 %collective-permute-start.14 = (f32[1,16,6,128]{3,1,2,0:T(8,128)S(1)}, f32[1,16,6,128]{3,1,2,0:T(8,128)S(1)}, u32[]{:S(2)}, u32[]{:S(2)}) collective-permute-start(f32[1,16,6,128]{3,1,2,0:T(8,128)S(1)} %get-tuple-element.53), channel_id=1, source_target_pairs={{1,0},{2,1},{3,2},{4,3},{5,4},{6,5},{7,6},{8,7},{9,8},{10,9},{11,1... | collective-permute-start | bytes 147464 | tf_op jit(solution)/shard_map/ppermute | solution.py:30
  102.9 8.2 %collective-permute-start.15 = (f32[1,16,6,128]{3,1,2,0:T(8,128)S(1)}, f32[1,16,6,128]{3,1,2,0:T(8,128)S(1)}, u32[]{:S(2)}, u32[]{:S(2)}) collective-permute-start(f32[1,16,6,128]{3,1,2,0:T(8,128)S(1)} %get-tuple-element.54), channel_id=1, source_target_pairs={{0,1},{1,2},{2,3},{3,4},{4,5},{5,6},{6,7},{7,8},{8,9},{9,10},{10,1... | collective-permute-start | bytes 147464 | tf_op jit(solution)/shard_map/ppermute | solution.py:27
  111.1 4.2 copy-start.4
  111.8 170.1 %copy-start.2 = (f32[1,16,12,128]{3,1,2,0:T(8,128)}, f32[1,16,12,128]{3,1,2,0:T(8,128)S(1)}, u32[]{:S(2)}) copy-start(f32[1,16,12,128]{3,1,2,0:T(8,128)S(1)} %get-tuple-element.7) | copy-start | bytes 294916
  112.7 165.3 %all-gather.9.cloned.1.call-start = ((), (), s32[]{:S(2)}) async-start(), calls=%async_computation.2 | async-start | bytes 3244032 | tf_op jit(solution)/shard_map/all_gather | solution.py:37
  113.5 235.6 %all-gather.11.cloned.1.call-start = ((), (), s32[]{:S(2)}) async-start(), calls=%async_computation.3 | async-start | bytes 3244032 | tf_op jit(solution)/shard_map/all_gather | solution.py:37
  114.4 305.2 %all-gather.5.cloned.1.call-start = ((), (), s32[]{:S(2)}) async-start(), calls=%async_computation | async-start | bytes 3244032 | tf_op jit(solution)/shard_map/all_gather | solution.py:37
Sparse Core Ops, SparseCore 0:
  112.8 94.6 all-gather.6
  209.6 68.3 all-gather.8
  280.8 68.3 all-gather.10
  351.2 68.3 all-gather.4
